TPU v7x, 32 devices: a whole 2x2x4 slice. The times are simulated.
32 devices in a mesh: grp: 2 (over x), ep: 8 (over z, y), dp: 2 (over core).
Axes of the slice: x: 2, y: 2, z: 4, core: 2. Of those that a mesh axis runs over, the one named last changes fastest.
Arguments:
- tokens: bfloat16 [2, 1024, 2048], P(None, ('grp', 'ep', 'dp')), parts along dimension 1, may hold values from -6 to 6
- norm_gain: float32 [2048], replicated, may hold values from 0.25 to 1.75
- expert_ids: int32 [2, 1024, 8], P(None, ('grp', 'ep', 'dp')), parts along dimension 1, may hold values from 0 to 15, all different within a row; in each aligned block of 32 rows (0 to 31, 32 to 63, ..., all dimensions but the last counted through in order) at most 24 rows name the same one
- gate_probs: float32 [2, 1024, 8], P(None, ('grp', 'ep', 'dp')), parts along dimension 1, may hold values from 0.05 to 1
- expert_weights: bfloat16 [16, 3, 2048, 768], P(('ep', 'dp')), may hold values from -0.125 to 0.125
Outputs:
- combined: bfloat16 [2, 1024, 2048], P(None, ('grp', 'ep', 'dp')), parts along dimension 1
There are 2 independent parts, one for each index of `grp`. A program takes and returns all parts, laid end to end along the dimension named above; an argument that names none is the same for every part. Nothing has to cross between parts.
Inputs may be any that keep to these rules, and one draw needn't show every extreme that they name: `expert_ids`: each token names 8 different experts. In each step the 32 tokens of one device (aligned blocks of 32 rows) name any one expert at most 24 times, a bound that some block reaches; every expert is named somewhere.
All inputs are finite; a program needn't handle non-finite values.
Results may differ from a plain program's by a relative error of at most 0.0072.
Values may be sent and summed in bfloat16 or wider, within the bound.
A program may use at most 128 MiB of HBM per device.

v0:
```python
import jax
import jax.numpy as jnp
from jax import lax
from jax.sharding import PartitionSpec as P

TOP = 8
BLOCK = 64


def norm_rows(hidden_rows, norm_gain):
    values = hidden_rows.astype(jnp.float32)
    inverse_rms = lax.rsqrt(jnp.mean(values * values, axis=-1, keepdims=True) + 1e-06)
    return (values * inverse_rms * norm_gain).astype(jnp.bfloat16)


def expert_rows(row_block, weights):
    gate_part = jnp.dot(row_block, weights[0], preferred_element_type=jnp.float32)
    up_part = jnp.dot(row_block, weights[1], preferred_element_type=jnp.float32)
    hidden = (jax.nn.silu(gate_part) * up_part).astype(jnp.bfloat16)
    return lax.dot_general(
        hidden, weights[2], (((1,), (1,)), ((), ())), preferred_element_type=jnp.float32
    )


def ragged_expert(inbound, arrived, weights):
    sources, capacity, width = inbound.shape
    slot_count = sources * capacity
    live_mask = lax.broadcasted_iota(jnp.int32, (sources, capacity), 1) < arrived[:, None]
    slot_order = jnp.argsort(1 - live_mask.reshape(slot_count).astype(jnp.int32), stable=True)
    slot_inverse = jnp.argsort(slot_order, stable=True)
    packed = inbound.reshape(slot_count, width)[slot_order]
    filled = jnp.sum(arrived)
    blocks_needed = (filled + BLOCK - 1) // BLOCK

    def one_block(number, result):
        offset = number * BLOCK
        section = lax.dynamic_slice_in_dim(packed, offset, BLOCK, 0)
        return lax.dynamic_update_slice_in_dim(result, expert_rows(section, weights), offset, 0)

    result = lax.fori_loop(0, blocks_needed, one_block, jnp.zeros((slot_count, width), jnp.float32))
    return result[slot_inverse].reshape(sources, capacity, width)


def route_step(normed, step_ids, experts, capacity):
    tok_count, width = normed.shape
    flat_ids = step_ids.reshape(-1)
    expert_hits = (flat_ids[:, None] == lax.broadcasted_iota(jnp.int32, (1, experts), 1)).astype(
        jnp.int32
    )
    earlier = jnp.cumsum(expert_hits, axis=0) - expert_hits
    slot_index = jnp.sum(earlier * expert_hits, axis=1)
    counts = jnp.sum(expert_hits, axis=0)
    target = flat_ids * capacity + slot_index
    pair_map = (
        target[:, None] == lax.broadcasted_iota(jnp.int32, (1, experts * capacity), 1)
    ).astype(jnp.bfloat16)
    token_map = jnp.sum(pair_map.reshape(tok_count, TOP, experts * capacity), axis=1)
    outbound = jnp.einsum(
        "tc,td->cd", token_map, normed, preferred_element_type=jnp.float32
    ).astype(jnp.bfloat16)
    return (outbound.reshape(experts, capacity, width), counts, pair_map)


def shards(tokens, norm_gain, expert_ids, gate_probs, expert_weights):
    ep_count = lax.axis_size("ep")
    dp_count = lax.axis_size("dp")
    experts = ep_count * dp_count
    steps_total, tok_count, width = tokens.shape
    capacity = 3 * tok_count * TOP // (2 * experts)
    weights = expert_weights[0]
    outputs = []
    for decode_step in range(steps_total):
        normed = norm_rows(tokens[decode_step], norm_gain)
        step_probs = gate_probs[decode_step]
        share = step_probs / jnp.sum(step_probs, axis=1, keepdims=True)
        outbound, counts, pair_map = route_step(normed, expert_ids[decode_step], experts, capacity)
        count_wire = counts.astype(jnp.bfloat16)
        inbound, inbound_counts = (
            lax.all_to_all(outbound, ("ep", "dp"), split_axis=0, concat_axis=0, tiled=True),
            lax.all_to_all(count_wire, ("ep", "dp"), split_axis=0, concat_axis=0, tiled=True),
        )
        arrived = inbound_counts.astype(jnp.int32)
        expert_out = ragged_expert(inbound, arrived, weights).astype(jnp.bfloat16)
        back_rows = lax.all_to_all(
            expert_out, ("ep", "dp"), split_axis=0, concat_axis=0, tiled=True
        )
        pair_values = jnp.dot(
            pair_map,
            back_rows.reshape(experts * capacity, width),
            preferred_element_type=jnp.float32,
        )
        mixed = jnp.sum(share[:, :, None] * pair_values.reshape(tok_count, TOP, width), axis=1)
        outputs.append(mixed.astype(jnp.bfloat16))
    return jnp.stack(outputs)


def solution(mesh):
    in_specs = (
        P(None, ("grp", "ep", "dp"), None),
        P(),
        P(None, ("grp", "ep", "dp"), None),
        P(None, ("grp", "ep", "dp"), None),
        P(("ep", "dp"), None, None, None),
    )
    out_specs = P(None, ("grp", "ep", "dp"), None)
    return jax.shard_map(shards, mesh=mesh, in_specs=in_specs, out_specs=out_specs, check_vma=False)
```

profile of v0, /device:TPU:15, one launch (start us, length us, event | category | flops | bytes accessed | tf_op | source)
XLA Modules:
  0.0 220.3 jit_solution(10256498972238891870)
XLA Ops:
  0.0 0.7 fusion.100
  0.7 0.1 copy.42
  0.8 0.1 eq.126
  0.9 0.1 eq.122
  1.0 0.6 reduce-window.14
  1.6 0.2 slice_reduce_fusion.1
  1.8 0.1 fusion.97
  1.9 0.7 copy.37
  2.6 6.6 %all-to-all-start = ((bf16[16,1,1]{2,1,0:T(2,128)(2,1)}), bf16[16,1,1]{2,1,0:T(2,128)(2,1)S(1)}, u32[]{:S(2)}, u32[]{:S(2)}) async-start(bf16[16,1,1]{2,1,0:T(2,128)(2,1)} %copy.37), calls=%async_computation | async-start | bytes 16384 | tf_op jit(solution)/shard_map/all_to_all | solution.py:80
  9.3 0.1 eq.141
  9.4 0.1 eq.137
  9.5 0.1 reduce_sum.138
  9.6 0.2 fusion.81
  9.8 1.1 fusion.74
  10.9 0.6 reduce-window.16
  11.5 0.2 slice_reduce_fusion
  11.7 0.1 fusion.96
  11.9 0.7 copy.41
  12.6 0.4 all-to-all-done
  13.0 6.0 %all-to-all-start.3 = ((bf16[16,1,1]{2,1,0:T(2,128)(2,1)}), bf16[16,1,1]{2,1,0:T(2,128)(2,1)S(1)}, u32[]{:S(2)}, u32[]{:S(2)}) async-start(bf16[16,1,1]{2,1,0:T(2,128)(2,1)} %copy.41), calls=%async_computation.3 | async-start | bytes 16384 | tf_op jit(solution)/shard_map/all_to_all | solution.py:80
  19.0 2.7 %convolution_convert_fusion.1 = bf16[384,2048]{1,0:T(8,128)(2,1)} fusion(bf16[32,384]{1,0:T(8,128)(2,1)S(1)} %fusion.81, f32[2048]{0:T(1024)} %param.10, f32[32]{0:T(128)S(1)} %get-tuple-element.108, bf16[2,32,2048]{2,1,0:T(8,128)(2,1)} %param.9), kind=kOutput, calls=%fused_computation.51 | convolution fusion | flops 51380224 | bytes 1736832 | tf_op jit(solution)/shard_map/tc,td->cd/dot_general | solution.py:58
  21.7 1.1 all-to-all-done.3
  22.8 6.4 %all-to-all-start.1 = ((bf16[16,24,2048]{2,1,0:T(8,128)(2,1)}), bf16[16,24,2048]{2,1,0:T(8,128)(2,1)S(1)}, u32[]{:S(2)}, u32[]{:S(2)}) async-start(bf16[16,24,2048]{2,1,0:T(8,128)(2,1)} %bitcast.13), calls=%async_computation.1 | async-start | bytes 3145728 | tf_op jit(solution)/shard_map/all_to_all | solution.py:79
  29.1 0.1 reduce_sum.146
  29.2 0.2 fusion.80
  29.5 1.8 convolution_convert_fusion
  31.2 0.9 convert_reduce_fusion.4
  32.8 0.9 convert_reduce_fusion.2
  34.5 0.1 sub.35
  34.7 0.1 sub.40
  34.8 3.8 %sort.59 = (s32[384]{0:T(512)}, s32[384]{0:T(512)S(1)}) sort(s32[384]{0:T(512)S(1)} %sub.35, s32[384]{0:T(512)S(1)} %iota.64), dimensions={0}, to_apply=%region_8.9 | sort | flops 3456 | bytes 6144 | tf_op jit(solution)/shard_map/jit(argsort)/sort | solution.py:29
  38.6 3.8 %sort.60 = (s32[384]{0:T(512)}, s32[384]{0:T(512)S(1)}) sort(s32[384]{0:T(512)S(1)} %get-tuple-element.65, s32[384]{0:T(512)S(1)} %iota.65), dimensions={0}, to_apply=%region_11.12 | sort | flops 3456 | bytes 6144 | tf_op jit(solution)/shard_map/jit(argsort)/sort | solution.py:30
  42.3 3.8 %sort.61 = (s32[384]{0:T(512)}, s32[384]{0:T(512)S(1)}) sort(s32[384]{0:T(512)S(1)} %sub.40, s32[384]{0:T(512)S(1)} %iota.67), dimensions={0}, to_apply=%region_21.22 | sort | flops 3456 | bytes 6144 | tf_op jit(solution)/shard_map/jit(argsort)/sort | solution.py:29
  46.1 3.8 %sort.62 = (s32[384]{0:T(512)}, s32[384]{0:T(512)S(1)}) sort(s32[384]{0:T(512)S(1)} %get-tuple-element.68, s32[384]{0:T(512)S(1)} %iota.68), dimensions={0}, to_apply=%region_24.25 | sort | flops 3456 | bytes 6144 | tf_op jit(solution)/shard_map/jit(argsort)/sort | solution.py:30
  50.0 15.4 %all-to-all-done.1 = bf16[16,24,2048]{2,1,0:T(8,128)(2,1)S(1)} async-done(((bf16[16,24,2048]{2,1,0:T(8,128)(2,1)}), bf16[16,24,2048]{2,1,0:T(8,128)(2,1)S(1)}, u32[]{:S(2)}, u32[]{:S(2)}) %all-to-all-start.1) | async-done | bytes 1572896 | tf_op jit(solution)/shard_map/all_to_all | solution.py:79
  65.3 4.9 %all-to-all-start.4 = ((bf16[16,24,2048]{2,1,0:T(8,128)(2,1)}), bf16[16,24,2048]{2,1,0:T(8,128)(2,1)S(1)}, u32[]{:S(2)}, u32[]{:S(2)}) async-start(bf16[16,24,2048]{2,1,0:T(8,128)(2,1)} %bitcast.125), calls=%async_computation.4 | async-start | bytes 3145728 | tf_op jit(solution)/shard_map/all_to_all | solution.py:79
  70.2 3.1 %gather_fusion = bf16[384,2048]{1,0:T(8,128)(2,1)} fusion(bf16[384,2048]{1,0:T(8,128)(2,1)S(1)} %bitcast.123, s32[1024]{0:T(1024)S(1)} %pad_clamp_fusion.3), kind=kCustom, calls=%fused_computation | custom fusion | bytes 3147264 | tf_op jit(solution)/shard_map/gather | solution.py:31
  73.4 0.2 broadcast.170.clone.1
  73.5 21.9 %while.20 = (s32[]{:T(128)}, bf16[384,2048]{1,0:T(8,128)(2,1)S(1)}, s32[]{:T(128)}, bf16[384,2048]{1,0:T(8,128)(2,1)}, bf16[3,2048,768]{2,1,0:T(8,128)(2,1)}, /*index=5*/s32[]{:T(128)}, s32[]{:T(128)}, s32[]{:T(128)}, s32[]{:T(128)}) while((s32[]{:T(128)}, bf16[384,2048]{1,0:T(8,128)(2,1)S(1)}, s32[]{:T(128)}, bf16[384,2048]{1,0:T(8,128)(2,1)}, ...), condition=%wide.region_10.11_spmd, body=%wide.region_9.10_spmd.sunk | while | flops 604274688 | bytes 10880143 | solution.py:40
  73.6 2.6 %fusion.124 = f32[64,768]{1,0:T(8,128)S(1)} fusion(bf16[3,2048,768]{2,1,0:T(8,128)(2,1)} %get-tuple-element.222, bf16[384,2048]{1,0:T(8,128)(2,1)} %get-tuple-element.221, s32[]{:T(128)S(6)} %select_n.40), kind=kOutput, calls=%fused_computation.8.clone.1 | convolution fusion | flops 201326592 | bytes 3604484 | tf_op jit(solution)/shard_map/while/body/dot_general | solution.py:17
  76.2 4.6 %fusion.125 = bf16[384,2048]{1,0:T(8,128)(2,1)S(1)} fusion(bf16[384,2048]{1,0:T(8,128)(2,1)S(1)} %get-tuple-element.210, s32[]{:T(128)S(6)} %select_n.40, bf16[3,2048,768]{2,1,0:T(8,128)(2,1)} %get-tuple-element.222, bf16[384,2048]{1,0:T(8,128)(2,1)} %get-tuple-element.221, f32[64,768]{1,0:T(8,128)S(1)} %fusion.124), kind=kOutput, calls=%fused_computation.13.clone.1 | convolution fusion | flops 402948096 | bytes 7275520 | tf_op jit(solution)/shard_map/while/body/dot_general | solution.py:20
  80.8 2.6 %fusion.124 = f32[64,768]{1,0:T(8,128)S(1)} fusion(bf16[3,2048,768]{2,1,0:T(8,128)(2,1)} %get-tuple-element.222, bf16[384,2048]{1,0:T(8,128)(2,1)} %get-tuple-element.221, s32[]{:T(128)S(6)} %select_n.40), kind=kOutput, calls=%fused_computation.8.clone.1 | convolution fusion | flops 201326592 | bytes 3604484 | tf_op jit(solution)/shard_map/while/body/dot_general | solution.py:17
  83.5 4.6 %fusion.125 = bf16[384,2048]{1,0:T(8,128)(2,1)S(1)} fusion(bf16[384,2048]{1,0:T(8,128)(2,1)S(1)} %get-tuple-element.210, s32[]{:T(128)S(6)} %select_n.40, bf16[3,2048,768]{2,1,0:T(8,128)(2,1)} %get-tuple-element.222, bf16[384,2048]{1,0:T(8,128)(2,1)} %get-tuple-element.221, f32[64,768]{1,0:T(8,128)S(1)} %fusion.124), kind=kOutput, calls=%fused_computation.13.clone.1 | convolution fusion | flops 402948096 | bytes 7275520 | tf_op jit(solution)/shard_map/while/body/dot_general | solution.py:20
  88.1 2.6 %fusion.124 = f32[64,768]{1,0:T(8,128)S(1)} fusion(bf16[3,2048,768]{2,1,0:T(8,128)(2,1)} %get-tuple-element.222, bf16[384,2048]{1,0:T(8,128)(2,1)} %get-tuple-element.221, s32[]{:T(128)S(6)} %select_n.40), kind=kOutput, calls=%fused_computation.8.clone.1 | convolution fusion | flops 201326592 | bytes 3604484 | tf_op jit(solution)/shard_map/while/body/dot_general | solution.py:17
  90.8 4.6 %fusion.125 = bf16[384,2048]{1,0:T(8,128)(2,1)S(1)} fusion(bf16[384,2048]{1,0:T(8,128)(2,1)S(1)} %get-tuple-element.210, s32[]{:T(128)S(6)} %select_n.40, bf16[3,2048,768]{2,1,0:T(8,128)(2,1)} %get-tuple-element.222, bf16[384,2048]{1,0:T(8,128)(2,1)} %get-tuple-element.221, f32[64,768]{1,0:T(8,128)S(1)} %fusion.124), kind=kOutput, calls=%fused_computation.13.clone.1 | convolution fusion | flops 402948096 | bytes 7275520 | tf_op jit(solution)/shard_map/while/body/dot_general | solution.py:20
  95.4 3.1 %gather_fusion.1 = bf16[384,2048]{1,0:T(8,128)(2,1)} fusion(bf16[384,2048]{1,0:T(8,128)(2,1)S(1)} %get-tuple-element.66, s32[1024]{0:T(1024)S(1)} %pad_clamp_fusion.2), kind=kCustom, calls=%fused_computation.1 | custom fusion | bytes 3147264 | tf_op jit(solution)/shard_map/gather | solution.py:41
  98.5 7.9 %all-to-all-done.4 = bf16[16,24,2048]{2,1,0:T(8,128)(2,1)S(1)} async-done(((bf16[16,24,2048]{2,1,0:T(8,128)(2,1)}), bf16[16,24,2048]{2,1,0:T(8,128)(2,1)S(1)}, u32[]{:S(2)}, u32[]{:S(2)}) %all-to-all-start.4) | async-done | bytes 1572896 | tf_op jit(solution)/shard_map/all_to_all | solution.py:79
  106.4 19.7 %all-to-all-start.2 = ((bf16[16,24,2048]{2,1,0:T(8,128)(2,1)}), bf16[16,24,2048]{2,1,0:T(8,128)(2,1)}, u32[]{:S(2)}, u32[]{:S(2)}) async-start(bf16[16,24,2048]{2,1,0:T(8,128)(2,1)} %bitcast.126), calls=%async_computation.2 | async-start | bytes 3145728 | tf_op jit(solution)/shard_map/all_to_all | solution.py:84
  126.2 3.1 %gather_fusion.2 = bf16[384,2048]{1,0:T(8,128)(2,1)} fusion(bf16[384,2048]{1,0:T(8,128)(2,1)S(1)} %bitcast.124, s32[1024]{0:T(1024)S(1)} %pad_clamp_fusion.1), kind=kCustom, calls=%fused_computation.2 | custom fusion | bytes 3147264 | tf_op jit(solution)/shard_map/gather | solution.py:31
  129.3 0.2 broadcast.170.clone
  129.4 22.0 %while.21 = (s32[]{:T(128)}, bf16[384,2048]{1,0:T(8,128)(2,1)S(1)}, s32[]{:T(128)}, bf16[384,2048]{1,0:T(8,128)(2,1)}, bf16[3,2048,768]{2,1,0:T(8,128)(2,1)}, /*index=5*/s32[]{:T(128)}, s32[]{:T(128)}, s32[]{:T(128)}, s32[]{:T(128)}) while((s32[]{:T(128)}, bf16[384,2048]{1,0:T(8,128)(2,1)S(1)}, s32[]{:T(128)}, ...), condition=%wide.region_23.24_spmd, body=%wide.region_22.23_spmd.sunk | while | flops 604274688 | bytes 10880143 | solution.py:40
  129.5 2.6 %fusion.131 = f32[64,768]{1,0:T(8,128)S(1)} fusion(bf16[3,2048,768]{2,1,0:T(8,128)(2,1)} %get-tuple-element.195, bf16[384,2048]{1,0:T(8,128)(2,1)} %get-tuple-element.194, s32[]{:T(128)S(6)} %select_n.41), kind=kOutput, calls=%fused_computation.31.clone.1 | convolution fusion | flops 201326592 | bytes 3604484 | tf_op jit(solution)/shard_map/while/body/dot_general | solution.py:17
  132.1 4.6 %fusion.132 = bf16[384,2048]{1,0:T(8,128)(2,1)S(1)} fusion(bf16[384,2048]{1,0:T(8,128)(2,1)S(1)} %get-tuple-element.183, s32[]{:T(128)S(6)} %select_n.41, bf16[3,2048,768]{2,1,0:T(8,128)(2,1)} %get-tuple-element.195, bf16[384,2048]{1,0:T(8,128)(2,1)} %get-tuple-element.194, f32[64,768]{1,0:T(8,128)S(1)} %fusion.131), kind=kOutput, calls=%fused_computation.36.clone.1 | convolution fusion | flops 402948096 | bytes 7275520 | tf_op jit(solution)/shard_map/while/body/dot_general | solution.py:20
  136.8 2.6 %fusion.131 = f32[64,768]{1,0:T(8,128)S(1)} fusion(bf16[3,2048,768]{2,1,0:T(8,128)(2,1)} %get-tuple-element.195, bf16[384,2048]{1,0:T(8,128)(2,1)} %get-tuple-element.194, s32[]{:T(128)S(6)} %select_n.41), kind=kOutput, calls=%fused_computation.31.clone.1 | convolution fusion | flops 201326592 | bytes 3604484 | tf_op jit(solution)/shard_map/while/body/dot_general | solution.py:17
  139.4 4.6 %fusion.132 = bf16[384,2048]{1,0:T(8,128)(2,1)S(1)} fusion(bf16[384,2048]{1,0:T(8,128)(2,1)S(1)} %get-tuple-element.183, s32[]{:T(128)S(6)} %select_n.41, bf16[3,2048,768]{2,1,0:T(8,128)(2,1)} %get-tuple-element.195, bf16[384,2048]{1,0:T(8,128)(2,1)} %get-tuple-element.194, f32[64,768]{1,0:T(8,128)S(1)} %fusion.131), kind=kOutput, calls=%fused_computation.36.clone.1 | convolution fusion | flops 402948096 | bytes 7275520 | tf_op jit(solution)/shard_map/while/body/dot_general | solution.py:20
  144.0 2.6 %fusion.131 = f32[64,768]{1,0:T(8,128)S(1)} fusion(bf16[3,2048,768]{2,1,0:T(8,128)(2,1)} %get-tuple-element.195, bf16[384,2048]{1,0:T(8,128)(2,1)} %get-tuple-element.194, s32[]{:T(128)S(6)} %select_n.41), kind=kOutput, calls=%fused_computation.31.clone.1 | convolution fusion | flops 201326592 | bytes 3604484 | tf_op jit(solution)/shard_map/while/body/dot_general | solution.py:17
  146.7 4.6 %fusion.132 = bf16[384,2048]{1,0:T(8,128)(2,1)S(1)} fusion(bf16[384,2048]{1,0:T(8,128)(2,1)S(1)} %get-tuple-element.183, s32[]{:T(128)S(6)} %select_n.41, bf16[3,2048,768]{2,1,0:T(8,128)(2,1)} %get-tuple-element.195, bf16[384,2048]{1,0:T(8,128)(2,1)} %get-tuple-element.194, f32[64,768]{1,0:T(8,128)S(1)} %fusion.131), kind=kOutput, calls=%fused_computation.36.clone.1 | convolution fusion | flops 402948096 | bytes 7275520 | tf_op jit(solution)/shard_map/while/body/dot_general | solution.py:20
  151.5 3.1 %gather_fusion.3 = bf16[384,2048]{1,0:T(8,128)(2,1)} fusion(bf16[384,2048]{1,0:T(8,128)(2,1)S(1)} %get-tuple-element.69, s32[1024]{0:T(1024)S(1)} %pad_clamp_fusion), kind=kCustom, calls=%fused_computation.3 | custom fusion | bytes 3147264 | tf_op jit(solution)/shard_map/gather | solution.py:41
  154.6 7.8 %all-to-all-done.2 = bf16[16,24,2048]{2,1,0:T(8,128)(2,1)} async-done(((bf16[16,24,2048]{2,1,0:T(8,128)(2,1)}), bf16[16,24,2048]{2,1,0:T(8,128)(2,1)}, u32[]{:S(2)}, u32[]{:S(2)}) %all-to-all-start.2) | async-done | bytes 1572896 | tf_op jit(solution)/shard_map/all_to_all | solution.py:84
  162.5 19.9 %all-to-all-start.5 = ((bf16[16,24,2048]{2,1,0:T(8,128)(2,1)}), bf16[16,24,2048]{2,1,0:T(8,128)(2,1)S(1)}, u32[]{:S(2)}, u32[]{:S(2)}) async-start(bf16[16,24,2048]{2,1,0:T(8,128)(2,1)} %bitcast.29), calls=%async_computation.5 | async-start | bytes 3145728 | tf_op jit(solution)/shard_map/all_to_all | solution.py:84
  182.6 2.4 %fusion.66 = bf16[32,2048]{1,0:T(8,128)(2,1)S(1)} fusion(bf16[384,2048,1]{1,0,2:T(8,128)(2,1)} %bitcast.18, f32[32,8]{1,0:T(8,128)S(1)} %copy.34, s32[32,8]{1,0:T(8,128)S(1)} %bitcast_add_fusion.1), kind=kOutput, calls=%fused_computation.54 | convolution fusion | flops 403734528 | bytes 1705984 | tf_op jit(solution)/shard_map/dot_general | solution.py:87
  185.0 33.6 %all-to-all-done.5 = bf16[16,24,2048]{2,1,0:T(8,128)(2,1)S(1)} async-done(((bf16[16,24,2048]{2,1,0:T(8,128)(2,1)}), bf16[16,24,2048]{2,1,0:T(8,128)(2,1)S(1)}, u32[]{:S(2)}, u32[]{:S(2)}) %all-to-all-start.5) | async-done | bytes 1572896 | tf_op jit(solution)/shard_map/all_to_all | solution.py:84
  218.5 1.0 fusion.67
  219.6 0.7 pad_maximum_fusion
  (36 shorter events, 0.6 us)
Async XLA Ops:
  2.6 10.4 %all-to-all-start = ((bf16[16,1,1]{2,1,0:T(2,128)(2,1)}), bf16[16,1,1]{2,1,0:T(2,128)(2,1)S(1)}, u32[]{:S(2)}, u32[]{:S(2)}) async-start(bf16[16,1,1]{2,1,0:T(2,128)(2,1)} %copy.37), calls=%async_computation | async-start | bytes 16384 | tf_op jit(solution)/shard_map/all_to_all | solution.py:80
  13.0 9.8 %all-to-all-start.3 = ((bf16[16,1,1]{2,1,0:T(2,128)(2,1)}), bf16[16,1,1]{2,1,0:T(2,128)(2,1)S(1)}, u32[]{:S(2)}, u32[]{:S(2)}) async-start(bf16[16,1,1]{2,1,0:T(2,128)(2,1)} %copy.41), calls=%async_computation.3 | async-start | bytes 16384 | tf_op jit(solution)/shard_map/all_to_all | solution.py:80
  22.8 6.7 %copy-start = (bf16[2,32,2048]{2,1,0:T(8,128)(2,1)S(1)}, bf16[2,32,2048]{2,1,0:T(8,128)(2,1)}, u32[]{:S(2)}) copy-start(bf16[2,32,2048]{2,1,0:T(8,128)(2,1)} %param.9) | copy-start | bytes 786436
  22.8 6.7 %copy-start.1 = (f32[2048]{0:T(1024)S(1)}, f32[2048]{0:T(1024)}, u32[]{:S(2)}) copy-start(f32[2048]{0:T(1024)} %param.10) | copy-start | bytes 24580
  22.8 42.6 %all-to-all-start.1 = ((bf16[16,24,2048]{2,1,0:T(8,128)(2,1)}), bf16[16,24,2048]{2,1,0:T(8,128)(2,1)S(1)}, u32[]{:S(2)}, u32[]{:S(2)}) async-start(bf16[16,24,2048]{2,1,0:T(8,128)(2,1)} %bitcast.13), calls=%async_computation.1 | async-start | bytes 3145728 | tf_op jit(solution)/shard_map/all_to_all | solution.py:79
  65.3 41.1 %all-to-all-start.4 = ((bf16[16,24,2048]{2,1,0:T(8,128)(2,1)}), bf16[16,24,2048]{2,1,0:T(8,128)(2,1)S(1)}, u32[]{:S(2)}, u32[]{:S(2)}) async-start(bf16[16,24,2048]{2,1,0:T(8,128)(2,1)} %bitcast.125), calls=%async_computation.4 | async-start | bytes 3145728 | tf_op jit(solution)/shard_map/all_to_all | solution.py:79
  106.4 56.0 %all-to-all-start.2 = ((bf16[16,24,2048]{2,1,0:T(8,128)(2,1)}), bf16[16,24,2048]{2,1,0:T(8,128)(2,1)}, u32[]{:S(2)}, u32[]{:S(2)}) async-start(bf16[16,24,2048]{2,1,0:T(8,128)(2,1)} %bitcast.126), calls=%async_computation.2 | async-start | bytes 3145728 | tf_op jit(solution)/shard_map/all_to_all | solution.py:84
  162.4 19.9 %copy-start.2 = (f32[2,32,8]{1,2,0:T(8,128)S(1)}, f32[2,32,8]{1,2,0:T(8,128)}, u32[]{:S(2)}) copy-start(f32[2,32,8]{1,2,0:T(8,128)} %param.12) | copy-start | bytes 6148
  162.5 56.1 %all-to-all-start.5 = ((bf16[16,24,2048]{2,1,0:T(8,128)(2,1)}), bf16[16,24,2048]{2,1,0:T(8,128)(2,1)S(1)}, u32[]{:S(2)}, u32[]{:S(2)}) async-start(bf16[16,24,2048]{2,1,0:T(8,128)(2,1)} %bitcast.29), calls=%async_computation.5 | async-start | bytes 3145728 | tf_op jit(solution)/shard_map/all_to_all | solution.py:84
where the time goes:
time: 221 us; the launch traced here: 220 us
  waiting for transfers between devices  66.2 us (30%)
  starting transfers between devices  63.5 us (29%)
  matrix products  51.4 us (23%)
  other arithmetic  21 us (10%)
  local copies, waits for them, and re-layouts  16.3 us (7%)
    all_to_all x2, waiting for transfers between devices, shards(): lax.all_to_all(expert_out, ('ep', 'dp'), split_axis=0, concat_axis=0, til...  41.4 us
    all_to_all x2, starting transfers between devices, shards(): lax.all_to_all(expert_out, ('ep', 'dp'), split_axis=0, concat_axis=0, til...  39.7 us
    dot_general x6, matrix products, expert_rows(): lax.dot_general(hidden, weights[2], (((1,), (1,)), ((), ())), preferred_e...  27.8 us
    all_to_all x2, waiting for transfers between devices, shards(): lax.all_to_all(outbound, ('ep', 'dp'), split_axis=0, concat_axis=0, tiled...  23.3 us
    dot_general x6, matrix products, expert_rows(): jnp.dot(row_block, weights[0], preferred_element_type=jnp.float32)  15.7 us
    all_to_all x2, starting transfers between devices, shards(): lax.all_to_all(count_wire, ('ep', 'dp'), split_axis=0, concat_axis=0, til...  12.6 us
    all_to_all x2, starting transfers between devices, shards(): lax.all_to_all(outbound, ('ep', 'dp'), split_axis=0, concat_axis=0, tiled...  11.3 us
    sort x2, other arithmetic, ragged_expert(): slot_inverse = jnp.argsort(slot_order, stable=True)  7.54 us
  transfers between devices with their start and end apart: 6, of which 6 were waited for; matrix products, arithmetic and copies ran while one was open for 38% of the time, Pallas kernels for 0%

commit v1 on v0

v1 whole, which is shorter than its diff:
```python
import jax
import jax.numpy as jnp
from jax import lax
from jax.sharding import PartitionSpec as P


def norm_rows(hidden_rows, norm_gain):
    values = hidden_rows.astype(jnp.float32)
    inverse_rms = lax.rsqrt(jnp.mean(values * values, axis=-1, keepdims=True) + 1e-06)
    return (values * inverse_rms * norm_gain).astype(jnp.bfloat16)


def expert_rows(row_block, weights):
    gate_part = jnp.dot(row_block, weights[0], preferred_element_type=jnp.float32)
    up_part = jnp.dot(row_block, weights[1], preferred_element_type=jnp.float32)
    hidden = (jax.nn.silu(gate_part) * up_part).astype(jnp.bfloat16)
    return lax.dot_general(
        hidden, weights[2], (((1,), (1,)), ((), ())), preferred_element_type=jnp.float32
    )


def shards(tokens, norm_gain, expert_ids, gate_probs, expert_weights):
    axes = ("ep", "dp")
    experts = lax.axis_size("ep") * lax.axis_size("dp")
    me = lax.axis_index(axes)
    steps_total, tok_count, width = tokens.shape
    rows = steps_total * tok_count
    normed = norm_rows(tokens.reshape(rows, width), norm_gain)
    share = gate_probs / jnp.sum(gate_probs, axis=-1, keepdims=True)
    hits = expert_ids[..., None] == lax.broadcasted_iota(jnp.int32, (1, 1, 1, experts), 3)
    dense_share = jnp.sum(jnp.where(hits, share[..., None], 0.0), axis=2).reshape(rows, experts)
    all_rows = lax.all_gather(normed, axes, tiled=True)
    all_share = lax.all_gather(dense_share, axes, tiled=True)
    mine = lax.broadcasted_iota(jnp.int32, (1, experts), 1) == me
    row_share = jnp.sum(jnp.where(mine, all_share, 0.0), axis=1, keepdims=True)
    expert_out = expert_rows(all_rows, expert_weights[0])
    weighted = (row_share * expert_out).astype(jnp.bfloat16)
    combined = lax.psum_scatter(weighted, axes, scatter_dimension=0, tiled=True)
    return combined.reshape(steps_total, tok_count, width)


def solution(mesh):
    in_specs = (
        P(None, ("grp", "ep", "dp"), None),
        P(),
        P(None, ("grp", "ep", "dp"), None),
        P(None, ("grp", "ep", "dp"), None),
        P(("ep", "dp"), None, None, None),
    )
    out_specs = P(None, ("grp", "ep", "dp"), None)
    return jax.shard_map(shards, mesh=mesh, in_specs=in_specs, out_specs=out_specs, check_vma=False)
```

time: 221 us -> 161 us (0.73)
  the two profiles are of different devices: /device:TPU:15 before, /device:TPU:0 now
where the time goes in v1:
time: 161 us; the launch traced here: 160 us
  waiting for transfers between devices  99.3 us (62%)
  blocking collectives  23.7 us (15%)
  matrix products  19 us (12%)
  between operations  13.4 us (8%)
  other arithmetic  4.5 us (3%)
    reduce_scatter x1, waiting for transfers between devices, shards(): combined = lax.psum_scatter(weighted, axes, scatter_dimension=0, tiled=True)  71.2 us
    all_gather x1, waiting for transfers between devices, shards(): all_rows = lax.all_gather(normed, axes, tiled=True)  28 us
    all_gather x1, blocking collectives, shards(): all_share = lax.all_gather(dense_share, axes, tiled=True)  23.7 us
    dot_general x1, matrix products, expert_rows(): lax.dot_general(hidden, weights[2], (((1,), (1,)), ((), ())), preferred_e...  12.8 us
    dot_general x1, matrix products, expert_rows(): up_part = jnp.dot(row_block, weights[1], preferred_element_type=jnp.float32)  6.13 us
  transfers between devices with their start and end apart: 2, of which 2 were waited for; matrix products, arithmetic and copies ran while one was open for 1% of the time, Pallas kernels for 0%

profile of v1, /device:TPU:0, one launch (start us, length us, event | category | flops | bytes accessed | tf_op | source)
XLA Modules:
  0.0 160.2 jit_solution(15941630990338274402)
XLA Ops:
  6.5 0.0 all-gather.3.cloned.1.call-start
  6.5 1.1 multiply_reduce_fusion
  7.6 0.1 rsqrt.12
  7.7 1.8 %fusion.13 = bf16[64,2048]{1,0:T(8,128)(2,1)} fusion(f32[2048]{0:T(1024)} %param.6, f32[64]{0:T(128)S(1)} %rsqrt.12, bf16[2,32,2048]{2,1,0:T(8,128)(2,1)} %param.5), kind=kLoop, calls=%fused_computation.12 | loop fusion | flops 524288 | bytes 532736 | tf_op jit(solution)/shard_map/convert_element_type | solution.py:10
  9.5 0.0 all-gather.3.cloned.1.call-update
  9.5 0.0 reduce-scatter.2.cloned.1.call-start
  9.6 0.8 fusion.15
  10.4 0.7 select_reduce_fusion
  11.1 0.1 reshape.45
  11.2 23.7 %all-gather = f32[16,64,16]{1,2,0:T(8,128)S(1)} all-gather(f32[1,64,16]{1,2,0:T(8,128)S(1)} %reshape.45), channel_id=1, replica_groups=mesh['grp'=2,'ep'=8,'dp'=2] {'ep','dp'}, dimensions={0}, use_global_device_ids=true | all-gather | bytes 69632 | tf_op jit(solution)/shard_map/all_gather | solution.py:33
  34.9 0.1 reshape.46
  35.0 0.1 select_reduce_fusion.1
  35.1 28.0 %all-gather.3.cloned.1.call-done = bf16[1024,2048]{1,0:T(8,128)(2,1)} async-done(((bf16[64,2048]{1,0:T(8,128)(2,1)}), bf16[1024,2048]{1,0:T(8,128)(2,1)}) %all-gather.3.cloned.1.call-update) | async-done | bytes 4194320 | tf_op jit(solution)/shard_map/all_gather | solution.py:32
  63.1 6.1 %fusion.1 = f32[1024,768]{1,0:T(8,128)S(1)} fusion(bf16[1024,2048]{1,0:T(8,128)(2,1)} %all-gather.3.cloned.1.call-done, bf16[1,3,2048,768]{3,2,1,0:T(8,128)(2,1)} %param.9), kind=kOutput, calls=%fused_computation.2 | convolution fusion | flops 3221225472 | bytes 10485760 | tf_op jit(solution)/shard_map/dot_general | solution.py:15
  69.3 12.8 %multiply_convert_fusion = bf16[1024,2048]{1,0:T(8,128)(2,1)} fusion(f32[1024]{0:T(1024)S(1)} %select_reduce_fusion.1, bf16[1,3,2048,768]{3,2,1,0:T(8,128)(2,1)} %param.9, f32[1024,768]{1,0:T(8,128)S(1)} %fusion.1, bf16[1024,2048]{1,0:T(8,128)(2,1)} %all-gather.3.cloned.1.call-done), kind=kOutput, calls=%fused_computation | convolution fusion | flops 6451363840 | bytes 17829888 | tf_op jit(solution)/shard_map/dot_general | solution.py:17
  82.1 0.0 reduce-scatter.2.cloned.1.call-update
  82.1 71.2 %reduce-scatter.2.cloned.1.call-done = bf16[64,2048]{1,0:T(8,128)(2,1)} async-done(((bf16[1024,2048]{1,0:T(8,128)(2,1)}), bf16[64,2048]{1,0:T(8,128)(2,1)}) %reduce-scatter.2.cloned.1.call-update) | async-done | bytes 262160 | tf_op jit(solution)/shard_map/reduce_scatter | solution.py:38
  (4 shorter events, 0.1 us)
Async XLA Ops:
  6.5 56.6 %all-gather.3.cloned.1.call-start = ((), (), s32[]{:S(2)}) async-start(), calls=%async_computation.1 | async-start | bytes 4456448 | tf_op jit(solution)/shard_map/all_gather | solution.py:32
  9.5 143.8 %reduce-scatter.2.cloned.1.call-start = ((), (), s32[]{:S(2)}) async-start(), calls=%async_computation.2 | async-start | bytes 4456448 | tf_op jit(solution)/shard_map/reduce_scatter | solution.py:38
Sparse Core Ops, SparseCore 0:
  9.7 53.4 all-gather.2
  82.2 71.0 reduce-scatter.1

commit v2 on v1

--- a/solution.py
+++ b/solution.py
@@ -1,7 +1,16 @@
+import functools
+
 import jax
 import jax.numpy as jnp
 from jax import lax
+from jax.experimental import pallas as pl
+from jax.experimental.pallas import tpu as pltpu
 from jax.sharding import PartitionSpec as P
+
+NZ = 4
+NY = 2
+LANES = 128
+B_LAG, D_LAG, E_LAG, END_LAG, INNER_LAG = 1, 2, 3, 6, 8
 
 
 def norm_rows(hidden_rows, norm_gain):
@@ -19,7 +28,7 @@
     )
 
 
-def shards(tokens, norm_gain, expert_ids, gate_probs, expert_weights):
+def gather_scatter_form(tokens, norm_gain, expert_ids, gate_probs, expert_weights):
     axes = ("ep", "dp")
     experts = lax.axis_size("ep") * lax.axis_size("dp")
     me = lax.axis_index(axes)
@@ -39,6 +48,337 @@
     return combined.reshape(steps_total, tok_count, width)
 
 
+def near_order(z, j):
+    high = z // 2
+    inner = z + high * (3 - 2 * z)
+    first = (3 - j) // 3
+    second = (j + 2) // 3 * ((4 - j) // 3)
+    k = j + inner * (first - second)
+    return k + high * (3 - 2 * k)
+
+
+def chain_order(z, g):
+    high = z // 2
+    inner = z + high * (3 - 2 * z)
+    k = (1 - inner) * (g + 1) + inner * ((g + 2) % 4)
+    return k + high * (3 - 2 * k)
+
+
+def moe_kernel(
+    tok_ref, gain_ref, ids_ref, prob_ref, w_hbm, out_ref,
+    x, wv, hid, ob, sr, ys, yr, zs, zr,
+    w_sem, x_recv, x_send, c_recv, c_send, y_recv, y_send, z_recv, z_send,
+):
+    steps, toks, width = tok_ref.shape
+    top = ids_ref.shape[2]
+    ff = wv.shape[2]
+    experts = lax.axis_size("ep") * lax.axis_size("dp")
+    ep = lax.axis_index("ep")
+    c = lax.axis_index("dp")
+    z = ep // NY
+    y = ep % NY
+    me = ep * 2 + c
+    groups = steps * NZ
+
+    sib = {"ep": ep, "dp": 1 - c}
+    ynb = {"ep": z * NY + 1 - y, "dp": c}
+    zup = {"ep": (z + 1) % NZ * NY + y, "dp": c}
+    zdn = {"ep": (z + NZ - 1) % NZ * NY + y, "dp": c}
+    can_up = z < NZ - 1
+    can_dn = z > 0
+    g_lag = jnp.where(can_up & can_dn, INNER_LAG, END_LAG)
+
+    for i in range(3):
+        pltpu.make_async_copy(w_hbm.at[0, i], wv.at[i], w_sem.at[i]).start()
+
+    barrier = pltpu.get_barrier_semaphore()
+    for peer in (sib, ynb):
+        pl.semaphore_signal(barrier, inc=1, device_id=peer)
+
+    @pl.when(can_up)
+    def _():
+        pl.semaphore_signal(barrier, inc=1, device_id=zup)
+
+    @pl.when(can_dn)
+    def _():
+        pl.semaphore_signal(barrier, inc=1, device_id=zdn)
+
+    def prepare(s):
+        x[s, z, c, y, :, :width] = norm_rows(tok_ref[s], gain_ref[...])
+        probs = prob_ref[s]
+        share = probs / jnp.sum(probs, axis=1, keepdims=True)
+        ids = ids_ref[s]
+        lane = lax.broadcasted_iota(jnp.int32, (toks, LANES), 1)
+        both = jnp.zeros((toks, LANES), jnp.float32)
+        for i in range(top):
+            named = ids[:, i : i + 1]
+            both = jnp.where(
+                (lane == named) | (lane == named + experts), share[:, i : i + 1], both
+            )
+        high = both.astype(jnp.bfloat16).astype(jnp.float32)
+        x[s, z, c, y, :, width:] = jnp.where(lane < experts, high, both - high).astype(jnp.bfloat16)
+
+    prepare(0)
+    pl.semaphore_wait(barrier, 2 + (z + NZ - 1) // NZ + (2 * (NZ - 1) - z) // NZ)
+
+    def x_copy(s, k, col, row, send, peer):
+        block = x.at[s, k, col, row]
+        return pltpu.make_async_remote_copy(
+            block, block, x_send.at[s, k, send], x_recv.at[s, k, col, row], device_id=peer
+        )
+
+    def relay_copies(s, k, act):
+        @pl.when((k <= z) & can_up)
+        def _():
+            act(x_copy(s, k, c, y, 0, zup))
+
+        @pl.when((k >= z) & can_dn)
+        def _():
+            act(x_copy(s, k, c, y, 1, zdn))
+
+        act(x_copy(s, k, c, y, 2, ynb))
+        act(x_copy(s, k, c, y, 3, sib))
+
+    def y_relay(s, k):
+        return x_copy(s, k, c, 1 - y, 4, sib)
+
+    def c_copy(s, k):
+        t = s * NZ + k
+        return pltpu.make_async_remote_copy(
+            ob.at[t, 1 - c], sr.at[t], c_send.at[t], c_recv.at[t], device_id=sib
+        )
+
+    def y_copy(s, k):
+        t = s * NZ + k
+        return pltpu.make_async_remote_copy(
+            ys.at[t], yr.at[t], y_send.at[t], y_recv.at[t], device_id=ynb
+        )
+
+    def z_copy(s, k, way, peer):
+        t = s * NZ + k
+        return pltpu.make_async_remote_copy(
+            zs.at[t], zr.at[s, way, k], z_send.at[t], z_recv.at[s, way, k], device_id=peer
+        )
+
+    def start(copy):
+        copy.start()
+
+    def finish(copy):
+        copy.wait_send()
+
+    def phase_a(t):
+        s, j = t // NZ, t % NZ
+        k = near_order(z, j)
+
+        @pl.when(j > 0)
+        def _():
+            x_copy(s, k, c, y, 2, ynb).wait_recv()
+
+        relay_copies(s, k, start)
+
+    def phase_b(t):
+        s, j = t // NZ, t % NZ
+        k = near_order(z, j)
+        x_copy(s, k, c, 1 - y, 2, ynb).wait_recv()
+        y_relay(s, k).start()
+
+    def phase_d(t):
+        s, j = t // NZ, t % NZ
+        k = near_order(z, j)
+
+        @pl.when(t == 0)
+        def _():
+            for i in range(3):
+                pltpu.make_async_copy(w_hbm.at[0, i], wv.at[i], w_sem.at[i]).wait()
+
+        for row in range(NY):
+            x_copy(s, k, 1 - c, row, 3, sib).wait_recv()
+        rows = 2 * NY * toks
+        lane = lax.broadcasted_iota(jnp.int32, (rows, LANES), 1)
+        pieces = x[s, k, :, :, :, width:].reshape(rows, LANES).astype(jnp.float32)
+        mine = (lane == me) | (lane == me + experts)
+        share = jnp.sum(jnp.where(mine, pieces, 0.0), axis=1, keepdims=True)
+        block = x[s, k, :, :, :, :width].reshape(rows, width)
+        tile = 256
+        for f in range(0, ff, tile):
+            gate = jnp.dot(block, wv[0, :, f : f + tile], preferred_element_type=jnp.float32)
+            up = jnp.dot(block, wv[1, :, f : f + tile], preferred_element_type=jnp.float32)
+            hid[:, f : f + tile] = (gate / (1.0 + jnp.exp(-gate)) * up).astype(jnp.bfloat16)
+        hidden = hid[...]
+        for d in range(0, width, tile):
+            part = lax.dot_general(
+                hidden, wv[2, d : d + tile, :], (((1,), (1,)), ((), ())),
+                preferred_element_type=jnp.float32,
+            )
+            ob[s * NZ + k, :, :, :, d : d + tile] = (
+                (share * part).astype(jnp.bfloat16).reshape(2, NY, toks, tile)
+            )
+        c_copy(s, k).start()
+
+    def f32(value):
+        return value.astype(jnp.float32)
+
+    def phase_e(t):
+        s, j = t // NZ, t % NZ
+        k = near_order(z, j)
+        n = s * NZ + k
+        c_copy(s, k).wait_recv()
+        ys[n] = (f32(ob[n, c, 1 - y]) + f32(sr[n, 1 - y])).astype(jnp.bfloat16)
+        y_copy(s, k).start()
+
+    def chip_sum(s, k):
+        n = s * NZ + k
+        return f32(ob[n, c, y]) + f32(sr[n, y]) + f32(yr[n])
+
+    def phase_g(s, g):
+        k = chain_order(z, g)
+        n = s * NZ + k
+        y_copy(s, k).wait_recv()
+
+        @pl.when(k > z)
+        def _():
+            @pl.when(can_dn)
+            def _():
+                z_copy(s, k, 0, zup).wait_recv()
+                zs[n] = (chip_sum(s, k) + f32(zr[s, 0, k])).astype(jnp.bfloat16)
+
+            @pl.when(z == 0)
+            def _():
+                zs[n] = chip_sum(s, k).astype(jnp.bfloat16)
+
+            z_copy(s, k, 0, zup).start()
+
+        @pl.when(k < z)
+        def _():
+            @pl.when(can_up)
+            def _():
+                z_copy(s, k, 1, zdn).wait_recv()
+                zs[n] = (chip_sum(s, k) + f32(zr[s, 1, k])).astype(jnp.bfloat16)
+
+            @pl.when(z == NZ - 1)
+            def _():
+                zs[n] = chip_sum(s, k).astype(jnp.bfloat16)
+
+            z_copy(s, k, 1, zdn).start()
+
+    def phase_h(s):
+        y_copy(s, z).wait_recv()
+
+        @pl.when(z == 0)
+        def _():
+            z_copy(s, z, 1, zdn).wait_recv()
+            out_ref[s] = (chip_sum(s, z) + f32(zr[s, 1, z])).astype(jnp.bfloat16)
+
+        @pl.when(z == NZ - 1)
+        def _():
+            z_copy(s, z, 0, zup).wait_recv()
+            out_ref[s] = (chip_sum(s, z) + f32(zr[s, 0, z])).astype(jnp.bfloat16)
+
+        @pl.when(can_up & can_dn)
+        def _():
+            z_copy(s, z, 0, zup).wait_recv()
+            z_copy(s, z, 1, zdn).wait_recv()
+            out_ref[s] = (
+                chip_sum(s, z) + f32(zr[s, 0, z]) + f32(zr[s, 1, z])
+            ).astype(jnp.bfloat16)
+
+    def slot_body(slot, carry):
+        @pl.when(slot < groups)
+        def _():
+            phase_a(slot)
+
+        @pl.when(slot == 0)
+        def _():
+            for s in range(1, steps):
+                prepare(s)
+
+        @pl.when((slot >= B_LAG) & (slot < groups + B_LAG))
+        def _():
+            phase_b(slot - B_LAG)
+
+        @pl.when((slot >= D_LAG) & (slot < groups + D_LAG))
+        def _():
+            phase_d(slot - D_LAG)
+
+        @pl.when((slot >= E_LAG) & (slot < groups + E_LAG))
+        def _():
+            phase_e(slot - E_LAG)
+
+        @pl.when((slot >= g_lag) & (slot < groups + g_lag))
+        def _():
+            t = slot - g_lag
+            s, g = t // NZ, t % NZ
+
+            @pl.when(g < NZ - 1)
+            def _():
+                phase_g(s, g)
+
+            @pl.when(g == NZ - 1)
+            def _():
+                phase_h(s)
+
+        return carry
+
+    lax.fori_loop(0, groups + INNER_LAG, slot_body, 0)
+
+    def drain(t, carry):
+        s, k = t // NZ, t % NZ
+        relay_copies(s, k, finish)
+        y_relay(s, k).wait_send()
+        c_copy(s, k).wait_send()
+        y_copy(s, k).wait_send()
+
+        @pl.when(k != z)
+        def _():
+            z_copy(s, k, 0, zup).wait_send()
+
+        return carry
+
+    lax.fori_loop(0, groups, drain, 0)
+
+
+def kernel_form(tokens, norm_gain, expert_ids, gate_probs, expert_weights):
+    steps, toks, width = tokens.shape
+    ff = expert_weights.shape[3]
+    groups = steps * NZ
+    half = jnp.bfloat16
+    vmem = pl.BlockSpec(memory_space=pltpu.VMEM)
+    dma = pltpu.SemaphoreType.DMA
+    rows = groups * 4 * toks
+    return pl.pallas_call(
+        moe_kernel,
+        out_shape=jax.ShapeDtypeStruct((steps, toks, width), half),
+        in_specs=[vmem, vmem, vmem, vmem, pl.BlockSpec(memory_space=pl.ANY)],
+        out_specs=vmem,
+        scratch_shapes=[
+            pltpu.VMEM((steps, NZ, 2, NY, toks, width + LANES), half),
+            pltpu.VMEM((3, width, ff), half),
+            pltpu.VMEM((4 * toks, ff), half),
+            pltpu.VMEM((groups, 2, NY, toks, width), half),
+            pltpu.VMEM((groups, NY, toks, width), half),
+            pltpu.VMEM((groups, toks, width), half),
+            pltpu.VMEM((groups, toks, width), half),
+            pltpu.VMEM((groups, toks, width), half),
+            pltpu.VMEM((steps, 2, NZ, toks, width), half),
+            dma((3,)),
+            dma((steps, NZ, 2, NY)),
+            dma((steps, NZ, 5)),
+            dma((groups,)),
+            dma((groups,)),
+            dma((groups,)),
+            dma((groups,)),
+            dma((steps, 2, NZ)),
+            dma((groups,)),
+        ],
+        compiler_params=pltpu.CompilerParams(
+            collective_id=0, has_side_effects=True, vmem_limit_bytes=48 * 1024 * 1024
+        ),
+        cost_estimate=pl.CostEstimate(
+            flops=6 * rows * width * ff, bytes_accessed=6 * width * ff, transcendentals=rows * ff
+        ),
+    )(tokens, norm_gain.reshape(1, width), expert_ids, gate_probs, expert_weights)
+
+
 def solution(mesh):
     in_specs = (
         P(None, ("grp", "ep", "dp"), None),
@@ -48,4 +388,6 @@
         P(("ep", "dp"), None, None, None),
     )
     out_specs = P(None, ("grp", "ep", "dp"), None)
+    small = mesh.shape["ep"] == NZ * NY and mesh.shape["dp"] == 2
+    shards = kernel_form if small else gather_scatter_form
     return jax.shard_map(shards, mesh=mesh, in_specs=in_specs, out_specs=out_specs, check_vma=False)

time: 161 us -> 82.6 us (0.51)
  waiting for transfers between devices: 99.3 us -> 0 us
  Pallas kernels: 0 us -> 78.3 us
  blocking collectives: 23.7 us -> 0 us
  matrix products: 19 us -> 0 us
  between operations: 13.4 us -> 0.02 us
  other arithmetic: 4.5 us -> 0 us
  local copies, waits for them, and re-layouts: 0.32 us -> 3.9 us
    pallas_call x0 -> x1, Pallas kernels: none -> 78.3 us  [kernel_form(): pl.pallas_call(moe_kernel, out_shape=jax.ShapeDtypeStruct((steps, toks, w...]
    reduce_scatter x1 -> x0, waiting for transfers between devices: 71.2 us -> none  [shards(): combined = lax.psum_scatter(weighted, axes, scatter_dimension=0, tiled=True)]
    all_gather x1 -> x0, waiting for transfers between devices: 28 us -> none  [shards(): all_rows = lax.all_gather(normed, axes, tiled=True)]
    all_gather x1 -> x0, blocking collectives: 23.7 us -> none  [shards(): all_share = lax.all_gather(dense_share, axes, tiled=True)]
    dot_general x2 -> x0, matrix products: 19 us -> none  [the longest x1 12.8 us: expert_rows(): lax.dot_general(hidden, weights[2], (((1,), (1,)), ((), ())), preferred_e...]
    unnamed x2 -> x7, local copies, waits for them, and re-layouts: 0.18 us -> 3.9 us
    reduce_sum x3 -> x0, other arithmetic: 1.89 us -> none  [the longest x1 1.08 us: norm_rows(): jnp.mean(values * values, axis=-1, keepdims=True) + 1e-06]
    convert_element_type x1 -> x0, other arithmetic: 1.81 us -> none  [norm_rows(): return (values * inverse_rms * norm_gain).astype(jnp.bfloat16)]
  transfers between devices with their start and end apart: 2 -> 0, of which waited for: 2 -> 0; matrix products, arithmetic and copies ran while one was open for 1% -> 0% of each run, Pallas kernels for 0% -> 0%
where the time goes in v2:
time: 82.6 us; the launch traced here: 82.2 us
  Pallas kernels  78.3 us (95%)
  local copies, waits for them, and re-layouts  3.9 us (5%)
    pallas_call x1, Pallas kernels, kernel_form(): pl.pallas_call(moe_kernel, out_shape=jax.ShapeDtypeStruct((steps, toks, w...  78.3 us
    unnamed x7, local copies, waits for them, and re-layouts  3.9 us

profile of v2, /device:TPU:0, one launch (start us, length us, event | category | flops | bytes accessed | tf_op | source)
XLA Modules:
  0.0 82.2 jit_solution(4693181619695305663)
XLA Ops:
  0.0 0.8 copy.6.ids_ref
  0.8 0.8 copy.7.prob_ref
  1.6 0.0 copy-start
  1.6 0.9 %copy-done = bf16[2,32,2048]{2,1,0:T(8,128)(2,1)S(1)} copy-done((bf16[2,32,2048]{2,1,0:T(8,128)(2,1)S(1)}, bf16[2,32,2048]{2,1,0:T(8,128)(2,1)}, u32[]{:S(2)}) %copy-start) | copy-done | bytes 262168
  2.5 0.0 copy-start.1
  2.5 0.7 copy-done.1
  3.2 78.3 %shard_map.55 = bf16[2,32,2048]{2,1,0:T(8,128)(2,1)S(1)} custom-call(bf16[2,32,2048]{2,1,0:T(8,128)(2,1)S(1)} %copy-done, f32[1,2048]{1,0:T(1,128)S(1)} %bitcast.1, s32[2,32,8]{2,1,0:T(8,128)S(1)} %copy.6.ids_ref, f32[2,32,8]{2,1,0:T(8,128)S(1)} %copy.7.prob_ref, bf16[1,3,2048,768]{3,2,1,0:T(8,128)(2,1)} %w_hbm.1), custom_call_target="tpu_custom_call" | custom-call | flops 9663676416 | bytes 9437184 | tf_op jit(solution)/shard_map/pallas_call | solution.py:348
  81.5 0.7 copy.9
Async XLA Ops:
  1.6 1.0 %copy-start = (bf16[2,32,2048]{2,1,0:T(8,128)(2,1)S(1)}, bf16[2,32,2048]{2,1,0:T(8,128)(2,1)}, u32[]{:S(2)}) copy-start(bf16[2,32,2048]{2,1,0:T(8,128)(2,1)} %tok_ref.1) | copy-start | bytes 786436
  2.5 0.7 copy-start.1

commit v3 on v2

--- a/solution.py
+++ b/solution.py
@@ -10,7 +10,7 @@
 NZ = 4
 NY = 2
 LANES = 128
-B_LAG, D_LAG, E_LAG, END_LAG, INNER_LAG = 1, 2, 3, 6, 8
+B_LAG, D_LAG, E_LAG, G_LAG = 1, 2, 3, 4
 
 
 def norm_rows(hidden_rows, norm_gain):
@@ -57,13 +57,6 @@
     return k + high * (3 - 2 * k)
 
 
-def chain_order(z, g):
-    high = z // 2
-    inner = z + high * (3 - 2 * z)
-    k = (1 - inner) * (g + 1) + inner * ((g + 2) % 4)
-    return k + high * (3 - 2 * k)
-
-
 def moe_kernel(
     tok_ref, gain_ref, ids_ref, prob_ref, w_hbm, out_ref,
     x, wv, hid, ob, sr, ys, yr, zs, zr,
@@ -86,7 +79,6 @@
     zdn = {"ep": (z + NZ - 1) % NZ * NY + y, "dp": c}
     can_up = z < NZ - 1
     can_dn = z > 0
-    g_lag = jnp.where(can_up & can_dn, INNER_LAG, END_LAG)
 
     for i in range(3):
         pltpu.make_async_copy(w_hbm.at[0, i], wv.at[i], w_sem.at[i]).start()
@@ -95,13 +87,9 @@
     for peer in (sib, ynb):
         pl.semaphore_signal(barrier, inc=1, device_id=peer)
 
-    @pl.when(can_up)
-    def _():
-        pl.semaphore_signal(barrier, inc=1, device_id=zup)
-
-    @pl.when(can_dn)
-    def _():
-        pl.semaphore_signal(barrier, inc=1, device_id=zdn)
+    for far in range(1, NZ):
+        peer = {"ep": (z + far) % NZ * NY + y, "dp": c}
+        pl.semaphore_signal(barrier, inc=1, device_id=peer)
 
     def prepare(s):
         x[s, z, c, y, :, :width] = norm_rows(tok_ref[s], gain_ref[...])
@@ -119,7 +107,7 @@
         x[s, z, c, y, :, width:] = jnp.where(lane < experts, high, both - high).astype(jnp.bfloat16)
 
     prepare(0)
-    pl.semaphore_wait(barrier, 2 + (z + NZ - 1) // NZ + (2 * (NZ - 1) - z) // NZ)
+    pl.semaphore_wait(barrier, NZ + 1)
 
     def x_copy(s, k, col, row, send, peer):
         block = x.at[s, k, col, row]
@@ -136,11 +124,22 @@
         def _():
             act(x_copy(s, k, c, y, 1, zdn))
 
-        act(x_copy(s, k, c, y, 2, ynb))
+        @pl.when((c == 0) | (k == z))
+        def _():
+            act(x_copy(s, k, c, y, 2, ynb))
+
         act(x_copy(s, k, c, y, 3, sib))
 
-    def y_relay(s, k):
-        return x_copy(s, k, c, 1 - y, 4, sib)
+    def far_copies(s, k, act):
+        @pl.when((c == 1) & (k <= z) & can_up)
+        def _():
+            act(x_copy(s, k, c, 1 - y, 4, zup))
+
+        @pl.when((c == 1) & (k >= z) & can_dn)
+        def _():
+            act(x_copy(s, k, c, 1 - y, 5, zdn))
+
+        act(x_copy(s, k, c, 1 - y, 6, sib))
 
     def c_copy(s, k):
         t = s * NZ + k
@@ -154,10 +153,11 @@
             ys.at[t], yr.at[t], y_send.at[t], y_recv.at[t], device_id=ynb
         )
 
-    def z_copy(s, k, way, peer):
+    def z_copy(s, k, place):
         t = s * NZ + k
         return pltpu.make_async_remote_copy(
-            zs.at[t], zr.at[s, way, k], z_send.at[t], z_recv.at[s, way, k], device_id=peer
+            zs.at[t], zr.at[s, place], z_send.at[t], z_recv.at[s, place],
+            device_id={"ep": k * NY + y, "dp": c},
         )
 
     def start(copy):
@@ -167,7 +167,7 @@
         copy.wait_send()
 
     def phase_a(t):
-        s, j = t // NZ, t % NZ
+        j, s = t // steps, t % steps
         k = near_order(z, j)
 
         @pl.when(j > 0)
@@ -177,13 +177,13 @@
         relay_copies(s, k, start)
 
     def phase_b(t):
-        s, j = t // NZ, t % NZ
+        j, s = t // steps, t % steps
         k = near_order(z, j)
         x_copy(s, k, c, 1 - y, 2, ynb).wait_recv()
-        y_relay(s, k).start()
+        far_copies(s, k, start)
 
     def phase_d(t):
-        s, j = t // NZ, t % NZ
+        j, s = t // steps, t % steps
         k = near_order(z, j)
 
         @pl.when(t == 0)
@@ -219,7 +219,7 @@
         return value.astype(jnp.float32)
 
     def phase_e(t):
-        s, j = t // NZ, t % NZ
+        j, s = t // steps, t % steps
         k = near_order(z, j)
         n = s * NZ + k
         c_copy(s, k).wait_recv()
@@ -230,57 +230,25 @@
         n = s * NZ + k
         return f32(ob[n, c, y]) + f32(sr[n, y]) + f32(yr[n])
 
-    def phase_g(s, g):
-        k = chain_order(z, g)
-        n = s * NZ + k
-        y_copy(s, k).wait_recv()
-
-        @pl.when(k > z)
-        def _():
-            @pl.when(can_dn)
-            def _():
-                z_copy(s, k, 0, zup).wait_recv()
-                zs[n] = (chip_sum(s, k) + f32(zr[s, 0, k])).astype(jnp.bfloat16)
-
-            @pl.when(z == 0)
-            def _():
-                zs[n] = chip_sum(s, k).astype(jnp.bfloat16)
-
-            z_copy(s, k, 0, zup).start()
-
-        @pl.when(k < z)
-        def _():
-            @pl.when(can_up)
-            def _():
-                z_copy(s, k, 1, zdn).wait_recv()
-                zs[n] = (chip_sum(s, k) + f32(zr[s, 1, k])).astype(jnp.bfloat16)
-
-            @pl.when(z == NZ - 1)
-            def _():
-                zs[n] = chip_sum(s, k).astype(jnp.bfloat16)
-
-            z_copy(s, k, 1, zdn).start()
+    def phase_g(t):
+        j, s = t // steps, t % steps
+        k = near_order(z, j)
+
+        @pl.when(j > 0)
+        def _():
+            y_copy(s, k).wait_recv()
+            zs[s * NZ + k] = chip_sum(s, k).astype(jnp.bfloat16)
+            z_copy(s, k, z).start()
 
     def phase_h(s):
         y_copy(s, z).wait_recv()
-
-        @pl.when(z == 0)
-        def _():
-            z_copy(s, z, 1, zdn).wait_recv()
-            out_ref[s] = (chip_sum(s, z) + f32(zr[s, 1, z])).astype(jnp.bfloat16)
-
-        @pl.when(z == NZ - 1)
-        def _():
-            z_copy(s, z, 0, zup).wait_recv()
-            out_ref[s] = (chip_sum(s, z) + f32(zr[s, 0, z])).astype(jnp.bfloat16)
-
-        @pl.when(can_up & can_dn)
-        def _():
-            z_copy(s, z, 0, zup).wait_recv()
-            z_copy(s, z, 1, zdn).wait_recv()
-            out_ref[s] = (
-                chip_sum(s, z) + f32(zr[s, 0, z]) + f32(zr[s, 1, z])
-            ).astype(jnp.bfloat16)
+        zr[s, z] = jnp.zeros(zr.shape[2:], zr.dtype)
+        for far in range(1, NZ):
+            z_copy(s, z, (z + far) % NZ).wait_recv()
+        total = chip_sum(s, z)
+        for place in range(NZ):
+            total = total + f32(zr[s, place])
+        out_ref[s] = total.astype(jnp.bfloat16)
 
     def slot_body(slot, carry):
         @pl.when(slot < groups)
@@ -304,33 +272,26 @@
         def _():
             phase_e(slot - E_LAG)
 
-        @pl.when((slot >= g_lag) & (slot < groups + g_lag))
-        def _():
-            t = slot - g_lag
-            s, g = t // NZ, t % NZ
-
-            @pl.when(g < NZ - 1)
-            def _():
-                phase_g(s, g)
-
-            @pl.when(g == NZ - 1)
-            def _():
-                phase_h(s)
+        @pl.when((slot >= G_LAG) & (slot < groups + G_LAG))
+        def _():
+            phase_g(slot - G_LAG)
 
         return carry
 
-    lax.fori_loop(0, groups + INNER_LAG, slot_body, 0)
+    lax.fori_loop(0, groups + G_LAG, slot_body, 0)
+    for s in range(steps):
+        phase_h(s)
 
     def drain(t, carry):
         s, k = t // NZ, t % NZ
         relay_copies(s, k, finish)
-        y_relay(s, k).wait_send()
+        far_copies(s, k, finish)
         c_copy(s, k).wait_send()
         y_copy(s, k).wait_send()
 
         @pl.when(k != z)
         def _():
-            z_copy(s, k, 0, zup).wait_send()
+            z_copy(s, k, z).wait_send()
 
         return carry
 
@@ -359,15 +320,15 @@
             pltpu.VMEM((groups, toks, width), half),
             pltpu.VMEM((groups, toks, width), half),
             pltpu.VMEM((groups, toks, width), half),
-            pltpu.VMEM((steps, 2, NZ, toks, width), half),
+            pltpu.VMEM((steps, NZ, toks, width), half),
             dma((3,)),
             dma((steps, NZ, 2, NY)),
-            dma((steps, NZ, 5)),
-            dma((groups,)),
-            dma((groups,)),
-            dma((groups,)),
-            dma((groups,)),
-            dma((steps, 2, NZ)),
+            dma((steps, NZ, 7)),
+            dma((groups,)),
+            dma((groups,)),
+            dma((groups,)),
+            dma((groups,)),
+            dma((steps, NZ)),
             dma((groups,)),
         ],
         compiler_params=pltpu.CompilerParams(

time: 82.6 us -> 70.6 us (0.85)
  Pallas kernels: 78.3 us -> 66.3 us
    pallas_call x1, Pallas kernels: 78.3 us -> 66.3 us  [kernel_form(): pl.pallas_call(moe_kernel, out_shape=jax.ShapeDtypeStruct((steps, toks, w...]
where the time goes in v3:
time: 70.6 us; the launch traced here: 70.3 us
  Pallas kernels  66.3 us (94%)
  local copies, waits for them, and re-layouts  3.9 us (6%)
    pallas_call x1, Pallas kernels, kernel_form(): pl.pallas_call(moe_kernel, out_shape=jax.ShapeDtypeStruct((steps, toks, w...  66.3 us
    unnamed x7, local copies, waits for them, and re-layouts  3.9 us

profile of v3, /device:TPU:0, one launch (start us, length us, event | category | flops | bytes accessed | tf_op | source)
XLA Modules:
  0.0 70.3 jit_solution(7494809627329087726)
XLA Ops:
  0.0 0.8 %copy.6.ids_ref = s32[2,32,8]{2,1,0:T(8,128)S(1)} copy(s32[2,32,8]{1,2,0:T(8,128)} %param.7) | data formatting | bytes 4096 | tf_op args[2]
  0.8 0.8 %copy.7.prob_ref = f32[2,32,8]{2,1,0:T(8,128)S(1)} copy(f32[2,32,8]{1,2,0:T(8,128)} %param.8) | data formatting | bytes 4096 | tf_op args[3]
  1.6 0.0 copy-start
  1.6 0.9 %copy-done = bf16[2,32,2048]{2,1,0:T(8,128)(2,1)S(1)} copy-done((bf16[2,32,2048]{2,1,0:T(8,128)(2,1)S(1)}, bf16[2,32,2048]{2,1,0:T(8,128)(2,1)}, u32[]{:S(2)}) %copy-start) | copy-done | bytes 262168
  2.5 0.0 copy-start.1
  2.5 0.7 copy-done.1
  3.2 66.3 %shard_map.55 = bf16[2,32,2048]{2,1,0:T(8,128)(2,1)S(1)} custom-call(bf16[2,32,2048]{2,1,0:T(8,128)(2,1)S(1)} %copy-done, f32[1,2048]{1,0:T(1,128)S(1)} %bitcast.1, s32[2,32,8]{2,1,0:T(8,128)S(1)} %copy.6.ids_ref, f32[2,32,8]{2,1,0:T(8,128)S(1)} %copy.7.prob_ref, bf16[1,3,2048,768]{3,2,1,0:T(8,128)(2,1)} %w_hbm.1), custom_call_target="tpu_custom_call" | custom-call | flops 9663676416 | bytes 9437184 | tf_op jit(solution)/shard_map/pallas_call | solution.py:309
  69.5 0.7 %copy.9 = bf16[2,32,2048]{2,1,0:T(8,128)(2,1)} copy(bf16[2,32,2048]{2,1,0:T(8,128)(2,1)S(1)} %shard_map.55) | data formatting | bytes 524288
Async XLA Ops:
  1.6 1.0 %copy-start = (bf16[2,32,2048]{2,1,0:T(8,128)(2,1)S(1)}, bf16[2,32,2048]{2,1,0:T(8,128)(2,1)}, u32[]{:S(2)}) copy-start(bf16[2,32,2048]{2,1,0:T(8,128)(2,1)} %tok_ref.1) | copy-start | bytes 786436
  2.5 0.7 copy-start.1

commit v4 on v3

--- a/solution.py
+++ b/solution.py
@@ -264,17 +264,17 @@
         def _():
             phase_b(slot - B_LAG)
 
+        @pl.when((slot >= G_LAG) & (slot < groups + G_LAG))
+        def _():
+            phase_g(slot - G_LAG)
+
+        @pl.when((slot >= E_LAG) & (slot < groups + E_LAG))
+        def _():
+            phase_e(slot - E_LAG)
+
         @pl.when((slot >= D_LAG) & (slot < groups + D_LAG))
         def _():
             phase_d(slot - D_LAG)
-
-        @pl.when((slot >= E_LAG) & (slot < groups + E_LAG))
-        def _():
-            phase_e(slot - E_LAG)
-
-        @pl.when((slot >= G_LAG) & (slot < groups + G_LAG))
-        def _():
-            phase_g(slot - G_LAG)
 
         return carry
 

time: 70.6 us -> 69.5 us (0.984)
  Pallas kernels: 66.3 us -> 65.2 us
    pallas_call x1, Pallas kernels: 66.3 us -> 65.2 us  [kernel_form(): pl.pallas_call(moe_kernel, out_shape=jax.ShapeDtypeStruct((steps, toks, w...]
where the time goes in v4:
time: 69.5 us; the launch traced here: 69.1 us
  Pallas kernels  65.2 us (94%)
  local copies, waits for them, and re-layouts  3.9 us (6%)
    pallas_call x1, Pallas kernels, kernel_form(): pl.pallas_call(moe_kernel, out_shape=jax.ShapeDtypeStruct((steps, toks, w...  65.2 us
    unnamed x7, local copies, waits for them, and re-layouts  3.9 us

profile of v4, /device:TPU:0, one launch (start us, length us, event | category | flops | bytes accessed | tf_op | source)
XLA Modules:
  0.0 69.1 jit_solution(178464015058060975)
XLA Ops:
  0.0 0.8 %copy.6.ids_ref = s32[2,32,8]{2,1,0:T(8,128)S(1)} copy(s32[2,32,8]{1,2,0:T(8,128)} %param.7) | data formatting | bytes 4096 | tf_op args[2]
  0.8 0.8 %copy.7.prob_ref = f32[2,32,8]{2,1,0:T(8,128)S(1)} copy(f32[2,32,8]{1,2,0:T(8,128)} %param.8) | data formatting | bytes 4096 | tf_op args[3]
  1.6 0.0 copy-start
  1.6 0.9 %copy-done = bf16[2,32,2048]{2,1,0:T(8,128)(2,1)S(1)} copy-done((bf16[2,32,2048]{2,1,0:T(8,128)(2,1)S(1)}, bf16[2,32,2048]{2,1,0:T(8,128)(2,1)}, u32[]{:S(2)}) %copy-start) | copy-done | bytes 262168
  2.5 0.0 copy-start.1
  2.5 0.7 %copy-done.1 = f32[2048]{0:T(1024)S(1)} copy-done((f32[2048]{0:T(1024)S(1)}, f32[2048]{0:T(1024)}, u32[]{:S(2)}) %copy-start.1) | copy-done | bytes 8216
  3.2 65.2 %shard_map.55 = bf16[2,32,2048]{2,1,0:T(8,128)(2,1)S(1)} custom-call(bf16[2,32,2048]{2,1,0:T(8,128)(2,1)S(1)} %copy-done, f32[1,2048]{1,0:T(1,128)S(1)} %bitcast.1, s32[2,32,8]{2,1,0:T(8,128)S(1)} %copy.6.ids_ref, f32[2,32,8]{2,1,0:T(8,128)S(1)} %copy.7.prob_ref, bf16[1,3,2048,768]{3,2,1,0:T(8,128)(2,1)} %w_hbm.1), custom_call_target="tpu_custom_call" | custom-call | flops 9663676416 | bytes 9437184 | tf_op jit(solution)/shard_map/pallas_call | solution.py:309
  68.4 0.7 %copy.9 = bf16[2,32,2048]{2,1,0:T(8,128)(2,1)} copy(bf16[2,32,2048]{2,1,0:T(8,128)(2,1)S(1)} %shard_map.55) | data formatting | bytes 524288
Async XLA Ops:
  1.6 1.0 %copy-start = (bf16[2,32,2048]{2,1,0:T(8,128)(2,1)S(1)}, bf16[2,32,2048]{2,1,0:T(8,128)(2,1)}, u32[]{:S(2)}) copy-start(bf16[2,32,2048]{2,1,0:T(8,128)(2,1)} %tok_ref.1) | copy-start | bytes 786436
  2.5 0.7 %copy-start.1 = (f32[2048]{0:T(1024)S(1)}, f32[2048]{0:T(1024)}, u32[]{:S(2)}) copy-start(f32[2048]{0:T(1024)} %param.6) | copy-start | bytes 24580
